TPU v7x, 32 devices: a whole 2x2x4 slice. The times are simulated.
32 devices in a mesh: dp: 8 (over z, x), tensor: 4 (over y, core).
Axes of the slice: x: 2, y: 2, z: 4, core: 2. Of those that a mesh axis runs over, the one named last changes fastest.
Arguments:
- inputs: bfloat16 [16, 1024, 768], P('dp'), may hold values from -6 to 6
- cotangent: bfloat16 [16, 1024, 768], P('dp', 'tensor'), may hold values from -6 to 6
- lengths: int32 [16], P('dp'), may hold values from 512 to 1024, as said below
- qkv_weight: bfloat16 [768, 3, 768], P(None, None, 'tensor'), may hold values from -0.21875 to 0.21875
- qkv_bias: bfloat16 [2, 768], P(None, 'tensor'), may hold values from -0.29882812 to 0.29882812
- out_weight: bfloat16 [768, 768], P('tensor'), may hold values from -4 to 4
- out_bias: bfloat16 [768], replicated, may hold values from -0.59765625 to 0.59765625
- first_gain: bfloat16 [768], replicated, may hold values from 0.5 to 1.5
- first_shift: bfloat16 [768], replicated, may hold values from -0.59765625 to 0.59765625
- up_weight: bfloat16 [768, 3072], P(None, 'tensor'), may hold values from -0.21875 to 0.21875
- up_bias: bfloat16 [3072], P('tensor'), may hold values from -0.59765625 to 0.59765625
- down_weight: bfloat16 [3072, 768], P('tensor'), may hold values from -0.109375 to 0.109375
- down_bias: bfloat16 [768], replicated, may hold values from -0.59765625 to 0.59765625
- second_gain: bfloat16 [768], replicated, may hold values from 0.5 to 1.5
- second_shift: bfloat16 [768], replicated, may hold values from -0.59765625 to 0.59765625
Outputs:
- outputs: bfloat16 [16, 1024, 768], P('dp', 'tensor')
- input_grad: bfloat16 [16, 1024, 768], P('dp', 'tensor')
- qkv_weight_grad: float32 [768, 3, 768], P('dp', None, 'tensor')
- qkv_bias_grad: float32 [2, 768], P(None, 'tensor')
- out_weight_grad: float32 [768, 768], P(('tensor', 'dp'))
- out_bias_grad: float32 [768], replicated
- first_gain_grad: float32 [768], replicated
- first_shift_grad: float32 [768], replicated
- up_weight_grad: float32 [768, 3072], P('dp', 'tensor')
- up_bias_grad: float32 [3072], P('tensor')
- down_weight_grad: float32 [3072, 768], P(('tensor', 'dp'))
- down_bias_grad: float32 [768], replicated
- second_gain_grad: float32 [768], replicated
- second_shift_grad: float32 [768], replicated
Inputs may be any that keep to these rules, and one draw needn't show every extreme that they name: `lengths`: each sequence has at least half of 1024 valid slots; in every draw some sequence has all 1024 slots valid and some has exactly half of 1024.
All inputs are finite; a program needn't handle non-finite values.
Results may differ from a plain program's by a relative error of at most 0.018.
Values may be sent and summed in bfloat16 or wider, within the bound.
No kernel may reach another device: no remote copies, remote signals or barrier semaphores. Data moves between devices by JAX's collectives and lax.ppermute only.
A program may use at most 192 MiB of HBM per device.

v0:
```python
import math
import jax
import jax.numpy as jnp
from jax import lax
from jax.sharding import PartitionSpec as P

HEAD = 64


def split_up(array, dim, peers):
    before, after = (array.shape[:dim], array.shape[dim + 1 :])
    return jnp.moveaxis(array.reshape(*before, peers, -1, *after), dim, 0)


def sent_and_summed(array, axis, dim):
    peers = lax.axis_size(axis)
    parts = lax.all_to_all(split_up(array, dim, peers), axis, 0, 0, tiled=True)
    return jnp.sum(parts.astype(jnp.float32), axis=0)


def in_one_piece(arrays, axis, dim, along):
    ends, at = ([], 0)
    for a in arrays[:-1]:
        at += a.shape[along]
        ends.append(at)
    both = jnp.concatenate(arrays, axis=along)
    return tuple(jnp.split(sent_and_summed(both, axis, dim), ends, axis=along))


def norm_rows(values, gain_row, shift_row):
    center = values - jnp.mean(values, axis=-1, keepdims=True)
    spread = jnp.mean(center * center, axis=-1, keepdims=True)
    return center * lax.rsqrt(spread + 1e-12) * gain_row + shift_row


def gelu_exact(values):
    return jax.nn.gelu(values, approximate=False)


def scores_for(query_part, key_rows, alive_cols):
    scores = jnp.einsum(
        "bhd,shd->hbs", query_part, key_rows, preferred_element_type=jnp.float32
    ) * (1.0 / math.sqrt(HEAD))
    return jnp.where(alive_cols[None, None, :], scores, -1e30)


def attend_forward(query_part, key_rows, value_rows, alive_cols):
    scores = scores_for(query_part, key_rows, alive_cols)
    row_max = jnp.max(scores, axis=-1, keepdims=True)
    exp_scores = jnp.exp(scores - row_max)
    row_total = jnp.sum(exp_scores, axis=-1, keepdims=True)
    soft_probs = (exp_scores / row_total).astype(jnp.bfloat16)
    context = jnp.einsum("hbs,shd->bhd", soft_probs, value_rows, preferred_element_type=jnp.float32)
    return (context, row_max + jnp.log(row_total))


def attend_backward(query_part, key_rows, value_rows, alive_cols, log_total, grad_context):
    scale = 1.0 / math.sqrt(HEAD)
    scores = scores_for(query_part, key_rows, alive_cols)
    soft_probs = jnp.exp(scores - log_total)
    probs_low = soft_probs.astype(jnp.bfloat16)
    grad_probs = jnp.einsum(
        "bhd,shd->hbs", grad_context, value_rows, preferred_element_type=jnp.float32
    )
    inner_sum = jnp.sum(soft_probs * grad_probs, axis=-1, keepdims=True)
    grad_scores = (soft_probs * (grad_probs - inner_sum)).astype(jnp.bfloat16)
    grad_query = (
        jnp.einsum("hbs,shd->bhd", grad_scores, key_rows, preferred_element_type=jnp.float32)
        * scale
    )
    grad_keys = (
        jnp.einsum("hbs,bhd->shd", grad_scores, query_part, preferred_element_type=jnp.float32)
        * scale
    )
    grad_values = jnp.einsum(
        "hbs,bhd->shd", probs_low, grad_context, preferred_element_type=jnp.float32
    )
    return (grad_query, grad_keys, grad_values)


def reduce_grads(groups):
    mat_grads, bias_grads, norm_grads = groups
    mat_sums = (
        sent_and_summed(mat_grads[0].astype(jnp.bfloat16), "dp", 0),
        sent_and_summed(mat_grads[1].astype(jnp.bfloat16), "dp", 0),
        *in_one_piece(
            (mat_grads[2].astype(jnp.bfloat16), mat_grads[3].astype(jnp.bfloat16)), "dp", 0, 1
        ),
    )
    bias_sums = lax.psum((bias_grads[0], bias_grads[1]), "dp")
    norm_sums = lax.psum(
        (norm_grads[0], norm_grads[1], norm_grads[2], norm_grads[3], norm_grads[4], norm_grads[5]),
        ("dp", "tensor"),
    )
    return (mat_sums, bias_sums, norm_sums)


def body(
    inputs,
    cotangent,
    lengths,
    qkv_weight,
    qkv_bias,
    out_weight,
    out_bias,
    first_gain,
    first_shift,
    up_weight,
    up_bias,
    down_weight,
    down_bias,
    second_gain,
    second_shift,
):
    seq_length = inputs.shape[1]
    local_width = out_weight.shape[0]
    local_heads = local_width // HEAD
    share_rows = cotangent.shape[1]
    block_rows = min(512, seq_length)
    row_start = lax.axis_index("tensor") * share_rows
    positions = jnp.arange(seq_length, dtype=jnp.int32)
    first_gain32 = first_gain.astype(jnp.float32)
    first_shift32 = first_shift.astype(jnp.float32)
    second_gain32 = second_gain.astype(jnp.float32)
    second_shift32 = second_shift.astype(jnp.float32)
    output_list = []
    input_list = []
    local_sum = None
    summed = None
    for micro_batch in range(inputs.shape[0]):
        tokens = inputs[micro_batch]
        alive_cols = positions < lengths[micro_batch]
        token_share = lax.dynamic_slice_in_dim(tokens, row_start, share_rows, 0).astype(jnp.float32)
        alive_share = lax.dynamic_slice_in_dim(alive_cols, row_start, share_rows, 0)
        projected = jnp.einsum(
            "sd,dkc->skc", tokens, qkv_weight, preferred_element_type=jnp.float32
        )
        query_rows = (
            (projected[:, 0] + qkv_bias[0])
            .astype(jnp.bfloat16)
            .reshape(seq_length, local_heads, HEAD)
        )
        key_rows = projected[:, 1].astype(jnp.bfloat16).reshape(seq_length, local_heads, HEAD)
        value_rows = (
            (projected[:, 2] + qkv_bias[1])
            .astype(jnp.bfloat16)
            .reshape(seq_length, local_heads, HEAD)
        )
        context_parts = []
        log_parts = []
        for block_start in range(0, seq_length, block_rows):
            context_part, log_part = attend_forward(
                query_rows[block_start : block_start + block_rows], key_rows, value_rows, alive_cols
            )
            context_parts.append(context_part)
            log_parts.append(log_part)
        context = (
            jnp.concatenate(context_parts, 0).reshape(seq_length, local_width).astype(jnp.bfloat16)
        )
        attention_share = lax.psum_scatter(
            jnp.dot(context, out_weight, preferred_element_type=jnp.float32).astype(jnp.bfloat16),
            "tensor",
            scatter_dimension=0,
            tiled=True,
        ).astype(jnp.float32)
        first_in = attention_share + out_bias + token_share
        first_norm, first_pull = jax.vjp(norm_rows, first_in, first_gain32, first_shift32)
        first_rows = lax.all_gather(first_norm.astype(jnp.bfloat16), "tensor", axis=0, tiled=True)
        hidden = jnp.dot(first_rows, up_weight, preferred_element_type=jnp.float32) + up_bias
        active = gelu_exact(hidden).astype(jnp.bfloat16)
        down_share = lax.psum_scatter(
            jnp.dot(active, down_weight, preferred_element_type=jnp.float32).astype(jnp.bfloat16),
            "tensor",
            scatter_dimension=0,
            tiled=True,
        ).astype(jnp.float32)
        second_in = down_share + down_bias + first_norm
        out_share, second_pull = jax.vjp(norm_rows, second_in, second_gain32, second_shift32)
        output_list.append(out_share.astype(jnp.bfloat16))
        seed_grad = jnp.where(alive_share[:, None], cotangent[micro_batch].astype(jnp.float32), 0.0)
        grad_second, grad_second_gain, grad_second_shift = second_pull(seed_grad)
        grad_down_rows = lax.all_gather(
            grad_second.astype(jnp.bfloat16), "tensor", axis=0, tiled=True
        )
        grad_active = lax.dot_general(
            grad_down_rows,
            down_weight,
            (((1,), (1,)), ((), ())),
            preferred_element_type=jnp.float32,
        )
        grad_down = lax.dot_general(
            active, grad_down_rows, (((0,), (0,)), ((), ())), preferred_element_type=jnp.float32
        )
        gelu_value, gelu_pull = jax.vjp(gelu_exact, hidden)
        grad_hidden = gelu_pull(grad_active)[0].astype(jnp.bfloat16)
        grad_up_bias = jnp.sum(grad_hidden, axis=0, dtype=jnp.float32)
        grad_up = lax.dot_general(
            first_rows, grad_hidden, (((0,), (0,)), ((), ())), preferred_element_type=jnp.float32
        )
        grad_first = (
            lax.psum_scatter(
                lax.dot_general(
                    grad_hidden,
                    up_weight,
                    (((1,), (1,)), ((), ())),
                    preferred_element_type=jnp.float32,
                ).astype(jnp.bfloat16),
                "tensor",
                scatter_dimension=0,
                tiled=True,
            ).astype(jnp.float32)
            + grad_second
        )
        grad_first_in, grad_first_gain, grad_first_shift = first_pull(grad_first)
        grad_attn_rows = lax.all_gather(
            grad_first_in.astype(jnp.bfloat16), "tensor", axis=0, tiled=True
        )
        grad_out = lax.dot_general(
            context, grad_attn_rows, (((0,), (0,)), ((), ())), preferred_element_type=jnp.float32
        )
        grad_context = lax.dot_general(
            grad_attn_rows, out_weight, (((1,), (1,)), ((), ())), preferred_element_type=jnp.float32
        )
        grad_context = grad_context.astype(jnp.bfloat16).reshape(seq_length, local_heads, HEAD)
        grad_keys = jnp.zeros((seq_length, local_heads, HEAD), jnp.float32)
        grad_values = jnp.zeros((seq_length, local_heads, HEAD), jnp.float32)
        query_grads = []
        for block_number, block_start in enumerate(range(0, seq_length, block_rows)):
            query_part_grad, key_part_grad, value_part_grad = attend_backward(
                query_rows[block_start : block_start + block_rows],
                key_rows,
                value_rows,
                alive_cols,
                log_parts[block_number],
                grad_context[block_start : block_start + block_rows],
            )
            query_grads.append(query_part_grad)
            grad_keys = grad_keys + key_part_grad
            grad_values = grad_values + value_part_grad
        grad_query = jnp.concatenate(query_grads, 0).reshape(seq_length, local_width)
        stacked = jnp.stack(
            [
                grad_query,
                grad_keys.reshape(seq_length, local_width),
                grad_values.reshape(seq_length, local_width),
            ],
            1,
        ).astype(jnp.bfloat16)
        grad_qkv = jnp.einsum("sd,skc->dkc", tokens, stacked, preferred_element_type=jnp.float32)
        grad_qkv_bias = jnp.stack(
            [
                jnp.sum(stacked[:, 0], axis=0, dtype=jnp.float32),
                jnp.sum(stacked[:, 2], axis=0, dtype=jnp.float32),
            ],
            0,
        )
        input_share = (
            lax.psum_scatter(
                jnp.einsum(
                    "skc,dkc->sd", stacked, qkv_weight, preferred_element_type=jnp.float32
                ).astype(jnp.bfloat16),
                "tensor",
                scatter_dimension=0,
                tiled=True,
            ).astype(jnp.float32)
            + grad_first_in
        )
        input_list.append(input_share.astype(jnp.bfloat16))
        micro_grads = (
            (grad_qkv, grad_out, grad_up, grad_down),
            (grad_qkv_bias, grad_up_bias),
            (
                jnp.sum(grad_first_in, axis=0),
                grad_first_gain,
                grad_first_shift,
                jnp.sum(grad_second, axis=0),
                grad_second_gain,
                grad_second_shift,
            ),
        )
        local_sum = (
            micro_grads if local_sum is None else jax.tree.map(jnp.add, local_sum, micro_grads)
        )
    summed = reduce_grads(local_sum)
    mat_sums, bias_sums, norm_sums = summed
    return (
        jnp.stack(output_list, 0),
        jnp.stack(input_list, 0),
        mat_sums[0],
        bias_sums[0],
        mat_sums[1],
        norm_sums[0],
        norm_sums[1],
        norm_sums[2],
        mat_sums[2],
        bias_sums[1],
        mat_sums[3],
        norm_sums[3],
        norm_sums[4],
        norm_sums[5],
    )


def solution(mesh):
    in_specs = (
        P("dp", None, None),
        P("dp", "tensor", None),
        P("dp"),
        P(None, None, "tensor"),
        P(None, "tensor"),
        P("tensor", None),
        P(),
        P(),
        P(),
        P(None, "tensor"),
        P("tensor"),
        P("tensor", None),
        P(),
        P(),
        P(),
    )
    out_specs = (
        P("dp", "tensor", None),
        P("dp", "tensor", None),
        P("dp", None, "tensor"),
        P(None, "tensor"),
        P(("tensor", "dp"), None),
        P(),
        P(),
        P(),
        P("dp", "tensor"),
        P("tensor"),
        P(("tensor", "dp"), None),
        P(),
        P(),
        P(),
    )
    return jax.shard_map(body, mesh=mesh, in_specs=in_specs, out_specs=out_specs, check_vma=False)
```

profile of v0, /device:TPU:0, one launch (start us, length us, event | category | flops | bytes accessed | tf_op | source)
XLA Modules:
  0.0 547.3 jit_solution(3790984775710877579)
XLA Ops:
  8.7 4.4 fusion.40
  49.0 13.5 %reduce-scatter.9.cloned.1.call-done = bf16[256,768]{1,0:T(8,128)(2,1)} async-done(((bf16[1024,768]{1,0:T(8,128)(2,1)}), bf16[256,768]{1,0:T(8,128)(2,1)}) %reduce-scatter.9.cloned.1.call-update) | async-done | bytes 393232 | tf_op jit(solution)/shard_map/reduce_scatter | solution.py:160
  62.5 30.9 %reduce-scatter.13.cloned.1.call-done = bf16[256,768]{1,0:T(8,128)(2,1)} async-done(((bf16[1024,768]{1,0:T(8,128)(2,1)}), bf16[256,768]{1,0:T(8,128)(2,1)}) %reduce-scatter.13.cloned.1.call-update) | async-done | bytes 393232 | tf_op jit(solution)/shard_map/reduce_scatter | solution.py:160
  101.9 17.7 %all-gather.9.cloned.1.call-done = bf16[1024,768]{1,0:T(8,128)(2,1)} async-done(((bf16[256,768]{1,0:T(8,128)(2,1)}), bf16[1024,768]{1,0:T(8,128)(2,1)}) %all-gather.9.cloned.1.call-update) | async-done | bytes 1572880 | tf_op jit(solution)/shard_map/all_gather | solution.py:168
  119.5 4.4 fusion.143
  124.0 17.2 %all-gather.7.cloned.1.call-done = bf16[1024,768]{1,0:T(8,128)(2,1)} async-done(((bf16[256,768]{1,0:T(8,128)(2,1)}), bf16[1024,768]{1,0:T(8,128)(2,1)}) %all-gather.7.cloned.1.call-update) | async-done | bytes 1572880 | tf_op jit(solution)/shard_map/all_gather | solution.py:168
  141.2 17.4 %multiply_convert_fusion.5 = (bf16[1024,768]{1,0:T(8,128)(2,1)S(1)}, f32[1024,768]{1,0:T(8,128)}, bf16[1024,768]{1,0:T(8,128)(2,1)}, f32[1024,768]{1,0:T(8,128)}, f32[1024,768]{1,0:T(8,128)}) fusion(f32[768]{0:T(1024)} %convert_element_type.280, f32[1024,768]{1,0:T(8,128)} %fusion.143, bf16[1024,768]{1,0:T(8,128)(2,1)} %all-gather.7.cloned.1.call-done, ...), kind=kOutput, calls=%fused_computation.64 | convolution fusion | flops 1311768576 | bytes 18484224 | tf_op jit(solution)/shard_map/dot_general | solution.py:169
  162.4 4.3 convolution_convert_fusion.2
  173.1 17.5 %reduce-scatter.11.cloned.1.call-done = bf16[256,768]{1,0:T(8,128)(2,1)} async-done(((bf16[1024,768]{1,0:T(8,128)(2,1)}), bf16[256,768]{1,0:T(8,128)(2,1)}) %reduce-scatter.11.cloned.1.call-update) | async-done | bytes 393232 | tf_op jit(solution)/shard_map/reduce_scatter | solution.py:171
  190.7 30.8 %reduce-scatter.15.cloned.1.call-done = bf16[256,768]{1,0:T(8,128)(2,1)} async-done(((bf16[1024,768]{1,0:T(8,128)(2,1)}), bf16[256,768]{1,0:T(8,128)(2,1)}) %reduce-scatter.15.cloned.1.call-update) | async-done | bytes 393232 | tf_op jit(solution)/shard_map/reduce_scatter | solution.py:171
  231.8 17.1 %all-gather.11.cloned.1.call-done = bf16[1024,768]{1,0:T(8,128)(2,1)} async-done(((bf16[256,768]{1,0:T(8,128)(2,1)}), bf16[1024,768]{1,0:T(8,128)(2,1)}) %all-gather.11.cloned.1.call-update) | async-done | bytes 1572880 | tf_op jit(solution)/shard_map/all_gather | solution.py:182
  248.9 4.8 fusion.144
  253.7 17.0 %all-gather.15.cloned.1.call-done = bf16[1024,768]{1,0:T(8,128)(2,1)} async-done(((bf16[256,768]{1,0:T(8,128)(2,1)}), bf16[1024,768]{1,0:T(8,128)(2,1)}) %all-gather.15.cloned.1.call-update) | async-done | bytes 1572880 | tf_op jit(solution)/shard_map/all_gather | solution.py:182
  270.7 11.5 %convert_reduce_fusion.1 = (f32[768]{0:T(1024)}, bf16[1024,768]{1,0:T(8,128)(2,1)}, f32[768]{0:T(1024)}, bf16[1024,768]{1,0:T(8,128)(2,1)S(1)}) fusion(f32[1024,768]{1,0:T(8,128)} %get-tuple-element.108, f32[1024,768]{1,0:T(8,128)} %fusion.143, f32[768]{0:T(1024)} %convert_element_type.280, f32[1024,768]{1,0:T(8,128)} %fusion.144, ...), kind=kOutput, calls=%fused_computation.43 | convolution fusion | flops 1234696704 | bytes 21636096 | tf_op jit(solution)/shard_map/dot_general | solution.py:185
  295.0 4.8 fusion.149
  299.9 14.5 %reduce-scatter.17.cloned.1.call-done = bf16[256,768]{1,0:T(8,128)(2,1)} async-done(((bf16[1024,768]{1,0:T(8,128)(2,1)}), bf16[256,768]{1,0:T(8,128)(2,1)}) %reduce-scatter.17.cloned.1.call-update) | async-done | bytes 393232 | tf_op jit(solution)/shard_map/reduce_scatter | solution.py:201
  314.4 30.7 %reduce-scatter.21.cloned.1.call-done = bf16[256,768]{1,0:T(8,128)(2,1)} async-done(((bf16[1024,768]{1,0:T(8,128)(2,1)}), bf16[256,768]{1,0:T(8,128)(2,1)}) %reduce-scatter.21.cloned.1.call-update) | async-done | bytes 393232 | tf_op jit(solution)/shard_map/reduce_scatter | solution.py:201
  360.7 4.3 copy.32
  365.0 5.6 %all-to-all-start.2 = ((bf16[8,96,1536]{2,1,0:T(8,128)(2,1)}), bf16[8,96,1536]{2,1,0:T(8,128)(2,1)}, u32[]{:S(2)}, u32[]{:S(2)}) async-start(bf16[8,96,1536]{2,1,0:T(8,128)(2,1)} %bitcast.251), calls=%async_computation.10 | async-start | bytes 4718592 | tf_op jit(solution)/shard_map/all_to_all | solution.py:17
  387.5 4.2 multiply_reduce_fusion.2
  434.6 5.8 %all-to-all-start.1 = ((bf16[8,24,768]{2,1,0:T(8,128)(2,1)}), bf16[8,24,768]{2,1,0:T(8,128)(2,1)}, u32[]{:S(2)}, u32[]{:S(2)}) async-start(bf16[8,24,768]{2,1,0:T(8,128)(2,1)} %bitcast.292), calls=%async_computation.9 | async-start | bytes 589824 | tf_op jit(solution)/shard_map/all_to_all | solution.py:17
  450.4 5.0 all-to-all-start
  457.6 45.9 %all-reduce = (f32[768]{0:T(1024)}, f32[768]{0:T(1024)}, f32[768]{0:T(1024)}, f32[768]{0:T(1024)}, f32[768]{0:T(1024)}, /*index=5*/f32[768]{0:T(1024)}) all-reduce(f32[768]{0:T(1024)S(1)} %add.359, f32[768]{0:T(1024)S(1)} %add.360, f32[768]{0:T(1024)S(1)} %add.361, ...), channel_id=1, replica_groups=mesh['dp'=8,'tensor'=4] {'dp','tensor'}, use_global_device_ids=true, to_apply=%region_45.46 | all-reduce | flops 4608 | bytes 36864 | tf_op jit(solution)/shard_map/psum | solution.py:91
  510.9 22.0 %all-reduce.1 = (f32[2,192]{1,0:T(2,128)}, f32[768]{0:T(1024)}) all-reduce(f32[2,192]{1,0:T(2,128)S(1)} %maximum_add_fusion, f32[768]{0:T(1024)S(1)} %add.364), channel_id=1, replica_groups=mesh['dp'=8,'tensor'=4] {'dp'}, use_global_device_ids=true, to_apply=%region_41.42 | all-reduce | flops 1152 | bytes 9216 | tf_op jit(solution)/shard_map/psum | solution.py:90
  (431 shorter events, 179.7 us)
Async XLA Ops:
  7.2 112.4 %copy-start = (bf16[768,768]{1,0:T(8,128)(2,1)S(1)}, bf16[768,768]{1,0:T(8,128)(2,1)}, u32[]{:S(2)}) copy-start(bf16[768,768]{1,0:T(8,128)(2,1)} %param.24) | copy-start | bytes 3538948
  7.2 55.3 %reduce-scatter.9.cloned.1.call-start = ((), (), s32[]{:S(2)}) async-start(), calls=%async_computation.11 | async-start | bytes 1966080 | tf_op jit(solution)/shard_map/reduce_scatter | solution.py:160
  31.5 61.9 %reduce-scatter.13.cloned.1.call-start = ((), (), s32[]{:S(2)}) async-start(), calls=%async_computation.14 | async-start | bytes 1966080 | tf_op jit(solution)/shard_map/reduce_scatter | solution.py:160
  45.1 74.5 %all-gather.9.cloned.1.call-start = ((), (), s32[]{:S(2)}) async-start(), calls=%async_computation.15 | async-start | bytes 1966080 | tf_op jit(solution)/shard_map/all_gather | solution.py:168
  49.0 172.4 %copy-start.12 = (bf16[1,1024,768]{2,1,0:T(8,128)(2,1)}, bf16[1,1024,768]{2,1,0:T(8,128)(2,1)S(1)}, u32[]{:S(2)}) copy-start(bf16[1,1024,768]{2,1,0:T(8,128)(2,1)S(1)} %get-tuple-element.80) | copy-start | bytes 4718596
  62.5 34.8 %copy-start.7 = (bf16[256,768]{1,0:T(8,128)(2,1)S(1)}, bf16[256,768]{1,0:T(8,128)(2,1)}, u32[]{:S(2)}) copy-start(bf16[256,768]{1,0:T(8,128)(2,1)} %reduce-scatter.9.cloned.1.call-done) | copy-start | bytes 1179652
  99.7 41.5 %all-gather.7.cloned.1.call-start = ((), (), s32[]{:S(2)}) async-start(), calls=%async_computation.12 | async-start | bytes 1966080 | tf_op jit(solution)/shard_map/all_gather | solution.py:168
  100.3 90.4 %reduce-scatter.11.cloned.1.call-start = ((), (), s32[]{:S(2)}) async-start(), calls=%async_computation.13 | async-start | bytes 1966080 | tf_op jit(solution)/shard_map/reduce_scatter | solution.py:171
  141.2 18.6 %copy-start.111 = (bf16[768,768]{1,0:T(8,128)(2,1)S(1)}, bf16[768,768]{1,0:T(8,128)(2,1)}, u32[]{:S(2)}) copy-start(bf16[768,768]{1,0:T(8,128)(2,1)} %param.26) | copy-start | bytes 3538948
  162.4 59.1 %reduce-scatter.15.cloned.1.call-start = ((), (), s32[]{:S(2)}) async-start(), calls=%async_computation.16 | async-start | bytes 1966080 | tf_op jit(solution)/shard_map/reduce_scatter | solution.py:171
  166.7 82.2 %all-gather.11.cloned.1.call-start = ((), (), s32[]{:S(2)}) async-start(), calls=%async_computation.17 | async-start | bytes 1966080 | tf_op jit(solution)/shard_map/all_gather | solution.py:182
  229.1 41.6 %all-gather.15.cloned.1.call-start = ((), (), s32[]{:S(2)}) async-start(), calls=%async_computation.21 | async-start | bytes 1966080 | tf_op jit(solution)/shard_map/all_gather | solution.py:182
  231.3 83.1 %reduce-scatter.17.cloned.1.call-start = ((), (), s32[]{:S(2)}) async-start(), calls=%async_computation.18 | async-start | bytes 1966080 | tf_op jit(solution)/shard_map/reduce_scatter | solution.py:201
  286.1 59.1 %reduce-scatter.21.cloned.1.call-start = ((), (), s32[]{:S(2)}) async-start(), calls=%async_computation.22 | async-start | bytes 1966080 | tf_op jit(solution)/shard_map/reduce_scatter | solution.py:201
  290.1 84.1 %all-gather.13.cloned.1.call-start = ((), (), s32[]{:S(2)}) async-start(), calls=%async_computation.19 | async-start | bytes 1966080 | tf_op jit(solution)/shard_map/all_gather | solution.py:215
  365.0 69.6 %all-to-all-start.2 = ((bf16[8,96,1536]{2,1,0:T(8,128)(2,1)}), bf16[8,96,1536]{2,1,0:T(8,128)(2,1)}, u32[]{:S(2)}, u32[]{:S(2)}) async-start(bf16[8,96,1536]{2,1,0:T(8,128)(2,1)} %bitcast.251), calls=%async_computation.10 | async-start | bytes 4718592 | tf_op jit(solution)/shard_map/all_to_all | solution.py:17
  370.7 23.8 %all-gather.17.cloned.1.call-start = ((), (), s32[]{:S(2)}) async-start(), calls=%async_computation.23 | async-start | bytes 1966080 | tf_op jit(solution)/shard_map/all_gather | solution.py:215
  374.0 162.9 %reduce-scatter.19.cloned.1.call-start = ((), (), s32[]{:S(2)}) async-start(), calls=%async_computation.20 | async-start | bytes 1966080 | tf_op jit(solution)/shard_map/reduce_scatter | solution.py:258
  410.9 127.2 %reduce-scatter.23.cloned.1.call-start = ((), (), s32[]{:S(2)}) async-start(), calls=%async_computation.24 | async-start | bytes 1966080 | tf_op jit(solution)/shard_map/reduce_scatter | solution.py:258
  434.6 15.9 %all-to-all-start.1 = ((bf16[8,24,768]{2,1,0:T(8,128)(2,1)}), bf16[8,24,768]{2,1,0:T(8,128)(2,1)}, u32[]{:S(2)}, u32[]{:S(2)}) async-start(bf16[8,24,768]{2,1,0:T(8,128)(2,1)} %bitcast.292), calls=%async_computation.9 | async-start | bytes 589824 | tf_op jit(solution)/shard_map/all_to_all | solution.py:17
  450.4 84.1 %all-to-all-start = ((bf16[8,96,3,192]{1,3,2,0:T(8,128)(2,1)}), bf16[8,96,3,192]{1,3,2,0:T(8,128)(2,1)}, u32[]{:S(2)}, u32[]{:S(2)}) async-start(bf16[8,96,3,192]{1,3,2,0:T(8,128)(2,1)} %copy.30), calls=%async_computation.8 | async-start | bytes 2359296 | tf_op jit(solution)/shard_map/all_to_all | solution.py:17
  505.5 31.4 %copy-start.14 = (f32[256,768]{1,0:T(8,128)S(1)}, f32[256,768]{1,0:T(8,128)}, u32[]{:S(2)}) copy-start(f32[256,768]{1,0:T(8,128)} %copy-done.13) | copy-start | bytes 2359300
  505.5 31.4 %copy-start.95 = (f32[256]{0:T(256)S(1)}, f32[256]{0:T(256)}, u32[]{:S(2)}) copy-start(f32[256]{0:T(256)} %copy-done.94) | copy-start | bytes 3076
  505.5 32.6 %copy-start.97 = (f32[256]{0:T(256)S(1)}, f32[256]{0:T(256)}, u32[]{:S(2)}) copy-start(f32[256]{0:T(256)} %copy-done.96) | copy-start | bytes 3076
  (121 other events, 481.8 us)
Sparse Core Ops, SparseCore 0:
  31.6 30.8 reduce-scatter.8
  65.2 28.1 reduce-scatter.12
  99.8 19.6 all-gather.8
  121.5 19.6 all-gather.6
  162.5 28.1 reduce-scatter.10
  193.2 28.1 reduce-scatter.14
  229.2 19.6 all-gather.10
  251.0 19.6 all-gather.14
  286.2 28.1 reduce-scatter.16
  316.9 28.1 reduce-scatter.20
  352.3 19.6 all-gather.12
  374.1 20.2 all-gather.16
  411.0 28.1 reduce-scatter.18
  441.8 28.6 reduce-scatter.22
where the time goes:
time: 556 us; the launch traced here: 547 us
  waiting for transfers between devices  212 us (38%)
  matrix products  131 us (24%)
  other arithmetic  68.8 us (12%)
  blocking collectives  67.8 us (12%)
  local copies, waits for them, and re-layouts  33.1 us (6%)
  starting transfers between devices  18.6 us (3%)
  between operations  16.2 us (3%)
    reduce_scatter x2, waiting for transfers between devices, body(): lax.psum_scatter(jnp.dot(active, down_weight, preferred_element_type=jnp....  48.3 us
    psum x1, blocking collectives, reduce_grads(): lax.psum((norm_grads[0], norm_grads[1], norm_grads[2], norm_grads[3], nor...  45.9 us
    reduce_scatter x2, waiting for transfers between devices, body(): lax.psum_scatter(lax.dot_general(grad_hidden, up_weight, (((1,), (1,)), (...  45.3 us
    reduce_scatter x2, waiting for transfers between devices, body(): lax.psum_scatter(jnp.dot(context, out_weight, preferred_element_type=jnp....  44.3 us
    all_gather x2, waiting for transfers between devices, body(): lax.all_gather(first_norm.astype(jnp.bfloat16), 'tensor', axis=0, tiled=T...  34.9 us
    all_gather x2, waiting for transfers between devices, body(): lax.all_gather(grad_second.astype(jnp.bfloat16), 'tensor', axis=0, tiled=...  34.1 us
    psum x1, blocking collectives, reduce_grads(): bias_sums = lax.psum((bias_grads[0], bias_grads[1]), 'dp')  22 us
    dot_general x2, matrix products, body(): jnp.dot(first_rows, up_weight, preferred_element_type=jnp.float32) + up_bias  21.8 us
  transfers between devices with their start and end apart: 17, of which 12 were waited for; matrix products, arithmetic and copies ran while one was open for 26% of the time, Pallas kernels for 0%

commit v1 on v0

--- a/solution.py
+++ b/solution.py
@@ -179,9 +179,24 @@
         output_list.append(out_share.astype(jnp.bfloat16))
         seed_grad = jnp.where(alive_share[:, None], cotangent[micro_batch].astype(jnp.float32), 0.0)
         grad_second, grad_second_gain, grad_second_shift = second_pull(seed_grad)
-        grad_down_rows = lax.all_gather(
-            grad_second.astype(jnp.bfloat16), "tensor", axis=0, tiled=True
-        )
+        x = grad_second.astype(jnp.bfloat16)
+        size, here, width = (lax.axis_size("tensor"), lax.axis_index("tensor"), x.shape[0])
+        right = [(i, (i + 1) % size) for i in range(size)]
+        left = [(i, (i - 1) % size) for i in range(size)]
+        grad_down_rows = jnp.zeros((*x.shape[:0], size * width, *x.shape[0 + 1 :]), x.dtype)
+        grad_down_rows = lax.dynamic_update_slice_in_dim(grad_down_rows, x, here * width, axis=0)
+        from_left = from_right = x
+        halfway = size // 2
+        for step in range(1, halfway + 1):
+            from_left = lax.ppermute(from_left, "tensor", right)
+            grad_down_rows = lax.dynamic_update_slice_in_dim(
+                grad_down_rows, from_left, (here - step) % size * width, axis=0
+            )
+            if step < size - halfway:
+                from_right = lax.ppermute(from_right, "tensor", left)
+                grad_down_rows = lax.dynamic_update_slice_in_dim(
+                    grad_down_rows, from_right, (here + step) % size * width, axis=0
+                )
         grad_active = lax.dot_general(
             grad_down_rows,
             down_weight,

time: 556 us -> 543 us (0.977)
  waiting for transfers between devices: 212 us -> 191 us
  local copies, waits for them, and re-layouts: 33.1 us -> 43.8 us
    all_gather x2 -> x0, waiting for transfers between devices: 34.1 us -> none  [body(): lax.all_gather(grad_second.astype(jnp.bfloat16), 'tensor', axis=0, tiled=...]
    ppermute x0 -> x6, waiting for transfers between devices: none -> 12.6 us  [the longest x4 12.6 us: body(): from_left = lax.ppermute(from_left, 'tensor', right)]
    dynamic_update_slice x0 -> x6, local copies, waits for them, and re-layouts: none -> 8.7 us  [the longest x4 5.13 us: body(): lax.dynamic_update_slice_in_dim(grad_down_rows, from_left, (here - step)...]
    dot_general x2, matrix products: 16.3 us -> 10.2 us  [body(): lax.dot_general(grad_down_rows, down_weight, (((1,), (1,)), ((), ())), pr...]
    unnamed x257 -> x267, local copies, waits for them, and re-layouts: 14.6 us -> 14 us
  transfers between devices with their start and end apart: 17 -> 21, of which waited for: 12 -> 13; matrix products, arithmetic and copies ran while one was open for 26% -> 28% of each run, Pallas kernels for 0% -> 0%
where the time goes in v1:
time: 543 us; the launch traced here: 534 us
  waiting for transfers between devices  191 us (35%)
  matrix products  127 us (23%)
  other arithmetic  67.9 us (13%)
  blocking collectives  67.9 us (13%)
  local copies, waits for them, and re-layouts  43.8 us (8%)
  starting transfers between devices  20.5 us (4%)
  between operations  16.2 us (3%)
    reduce_scatter x2, waiting for transfers between devices, body(): lax.psum_scatter(jnp.dot(active, down_weight, preferred_element_type=jnp....  48.2 us
    reduce_scatter x2, waiting for transfers between devices, body(): lax.psum_scatter(lax.dot_general(grad_hidden, up_weight, (((1,), (1,)), (...  46.9 us
    psum x1, blocking collectives, reduce_grads(): lax.psum((norm_grads[0], norm_grads[1], norm_grads[2], norm_grads[3], nor...  45.9 us
    reduce_scatter x2, waiting for transfers between devices, body(): lax.psum_scatter(jnp.dot(context, out_weight, preferred_element_type=jnp....  44.3 us
    all_gather x2, waiting for transfers between devices, body(): lax.all_gather(first_norm.astype(jnp.bfloat16), 'tensor', axis=0, tiled=T...  34.7 us
    psum x1, blocking collectives, reduce_grads(): bias_sums = lax.psum((bias_grads[0], bias_grads[1]), 'dp')  22 us
    dot_general x2, matrix products, body(): jnp.dot(first_rows, up_weight, preferred_element_type=jnp.float32) + up_bias  21.9 us
    all_to_all x3, starting transfers between devices, sent_and_summed(): parts = lax.all_to_all(split_up(array, dim, peers), axis, 0, 0, tiled=True)  16.2 us
  transfers between devices with their start and end apart: 21, of which 13 were waited for; matrix products, arithmetic and copies ran while one was open for 28% of the time, Pallas kernels for 0%

profile of v1, /device:TPU:0, one launch (start us, length us, event | category | flops | bytes accessed | tf_op | source)
XLA Modules:
  0.0 534.2 jit_solution(17178654032528646017)
XLA Ops:
  8.7 4.3 fusion.40
  49.1 13.4 %reduce-scatter.9.cloned.1.call-done = bf16[256,768]{1,0:T(8,128)(2,1)} async-done(((bf16[1024,768]{1,0:T(8,128)(2,1)}), bf16[256,768]{1,0:T(8,128)(2,1)}) %reduce-scatter.9.cloned.1.call-update) | async-done | bytes 393232 | tf_op jit(solution)/shard_map/reduce_scatter | solution.py:160
  62.5 30.9 %reduce-scatter.13.cloned.1.call-done = bf16[256,768]{1,0:T(8,128)(2,1)} async-done(((bf16[1024,768]{1,0:T(8,128)(2,1)}), bf16[256,768]{1,0:T(8,128)(2,1)}) %reduce-scatter.13.cloned.1.call-update) | async-done | bytes 393232 | tf_op jit(solution)/shard_map/reduce_scatter | solution.py:160
  102.1 17.4 %all-gather.7.cloned.1.call-done = bf16[1024,768]{1,0:T(8,128)(2,1)} async-done(((bf16[256,768]{1,0:T(8,128)(2,1)}), bf16[1024,768]{1,0:T(8,128)(2,1)}) %all-gather.7.cloned.1.call-update) | async-done | bytes 1572880 | tf_op jit(solution)/shard_map/all_gather | solution.py:168
  119.5 4.4 fusion.143
  123.9 17.3 %all-gather.5.cloned.1.call-done = bf16[1024,768]{1,0:T(8,128)(2,1)} async-done(((bf16[256,768]{1,0:T(8,128)(2,1)}), bf16[1024,768]{1,0:T(8,128)(2,1)}) %all-gather.5.cloned.1.call-update) | async-done | bytes 1572880 | tf_op jit(solution)/shard_map/all_gather | solution.py:168
  141.2 17.4 %multiply_convert_fusion.5 = (bf16[1024,768]{1,0:T(8,128)(2,1)S(1)}, f32[1024,768]{1,0:T(8,128)}, bf16[1024,768]{1,0:T(8,128)(2,1)}, f32[1024,768]{1,0:T(8,128)}, f32[1024,768]{1,0:T(8,128)}) fusion(f32[768]{0:T(1024)} %convert_element_type.280, f32[1024,768]{1,0:T(8,128)} %fusion.143, bf16[1024,768]{1,0:T(8,128)(2,1)} %all-gather.5.cloned.1.call-done, ...), kind=kOutput, calls=%fused_computation.64 | convolution fusion | flops 1311768576 | bytes 18484224 | tf_op jit(solution)/shard_map/dot_general | solution.py:169
  162.4 4.4 convolution_convert_fusion.2
  173.2 17.5 %reduce-scatter.11.cloned.1.call-done = bf16[256,768]{1,0:T(8,128)(2,1)} async-done(((bf16[1024,768]{1,0:T(8,128)(2,1)}), bf16[256,768]{1,0:T(8,128)(2,1)}) %reduce-scatter.11.cloned.1.call-update) | async-done | bytes 393232 | tf_op jit(solution)/shard_map/reduce_scatter | solution.py:171
  190.7 30.8 %reduce-scatter.15.cloned.1.call-done = bf16[256,768]{1,0:T(8,128)(2,1)} async-done(((bf16[1024,768]{1,0:T(8,128)(2,1)}), bf16[256,768]{1,0:T(8,128)(2,1)}) %reduce-scatter.15.cloned.1.call-update) | async-done | bytes 393232 | tf_op jit(solution)/shard_map/reduce_scatter | solution.py:171
  234.1 4.0 collective-permute-done
  238.1 8.4 %collective-permute-done.3 = bf16[256,768]{1,0:T(8,128)(2,1)} collective-permute-done((bf16[256,768]{1,0:T(8,128)(2,1)}, bf16[256,768]{1,0:T(8,128)(2,1)}, u32[]{:S(2)}, u32[]{:S(2)}) %collective-permute-start.3) | collective-permute-done | bytes 393248 | tf_op jit(solution)/shard_map/ppermute | solution.py:191
  259.4 7.1 %convert_reduce_fusion.1 = (f32[768]{0:T(1024)}, bf16[1024,768]{1,0:T(8,128)(2,1)}, f32[768]{0:T(1024)}, bf16[1024,768]{1,0:T(8,128)(2,1)S(1)}) fusion(f32[1024,768]{1,0:T(8,128)S(1)} %copy-done.123, f32[1024,768]{1,0:T(8,128)S(1)} %copy-done.116, f32[768]{0:T(1024)S(1)} %copy-done.102, f32[1024,768]{1,0:T(8,128)S(1)} %fusion.144, ...), kind=kOutput, calls=%fused_computation.43 | convolution fusion | flops 1234696704 | bytes 21636096 | tf_op jit(solution)/shard_map/dot_general | solution.py:200
  279.1 5.0 fusion.149
  284.1 16.0 %reduce-scatter.17.cloned.1.call-done = bf16[256,768]{1,0:T(8,128)(2,1)} async-done(((bf16[1024,768]{1,0:T(8,128)(2,1)}), bf16[256,768]{1,0:T(8,128)(2,1)}) %reduce-scatter.17.cloned.1.call-update) | async-done | bytes 393232 | tf_op jit(solution)/shard_map/reduce_scatter | solution.py:216
  300.1 30.9 %reduce-scatter.21.cloned.1.call-done = bf16[256,768]{1,0:T(8,128)(2,1)} async-done(((bf16[1024,768]{1,0:T(8,128)(2,1)}), bf16[256,768]{1,0:T(8,128)(2,1)}) %reduce-scatter.21.cloned.1.call-update) | async-done | bytes 393232 | tf_op jit(solution)/shard_map/reduce_scatter | solution.py:216
  347.7 4.3 copy.32
  352.0 5.6 %all-to-all-start.2 = ((bf16[8,96,1536]{2,1,0:T(8,128)(2,1)}), bf16[8,96,1536]{2,1,0:T(8,128)(2,1)}, u32[]{:S(2)}, u32[]{:S(2)}) async-start(bf16[8,96,1536]{2,1,0:T(8,128)(2,1)} %bitcast.251), calls=%async_computation.10 | async-start | bytes 4718592 | tf_op jit(solution)/shard_map/all_to_all | solution.py:17
  374.6 4.2 multiply_reduce_fusion.2
  384.2 4.1 fusion.62
  421.7 5.7 %all-to-all-start.1 = ((bf16[8,24,768]{2,1,0:T(8,128)(2,1)}), bf16[8,24,768]{2,1,0:T(8,128)(2,1)}, u32[]{:S(2)}, u32[]{:S(2)}) async-start(bf16[8,24,768]{2,1,0:T(8,128)(2,1)} %bitcast.292), calls=%async_computation.9 | async-start | bytes 589824 | tf_op jit(solution)/shard_map/all_to_all | solution.py:17
  437.4 4.8 all-to-all-start
  444.4 45.9 %all-reduce = (f32[768]{0:T(1024)}, f32[768]{0:T(1024)}, f32[768]{0:T(1024)}, f32[768]{0:T(1024)}, f32[768]{0:T(1024)}, /*index=5*/f32[768]{0:T(1024)}) all-reduce(f32[768]{0:T(1024)S(1)} %add.399, f32[768]{0:T(1024)S(1)} %add.400, f32[768]{0:T(1024)S(1)} %add.401, ...), channel_id=1, replica_groups=mesh['dp'=8,'tensor'=4] {'dp','tensor'}, use_global_device_ids=true, to_apply=%region_45.46 | all-reduce | flops 4608 | bytes 36864 | tf_op jit(solution)/shard_map/psum | solution.py:91
  497.8 22.0 %all-reduce.1 = (f32[2,192]{1,0:T(2,128)}, f32[768]{0:T(1024)}) all-reduce(f32[2,192]{1,0:T(2,128)S(1)} %maximum_add_fusion, f32[768]{0:T(1024)S(1)} %add.404), channel_id=1, replica_groups=mesh['dp'=8,'tensor'=4] {'dp'}, use_global_device_ids=true, to_apply=%region_41.42 | all-reduce | flops 1152 | bytes 9216 | tf_op jit(solution)/shard_map/psum | solution.py:90
  (455 shorter events, 192.1 us)
Async XLA Ops:
  7.2 112.3 %copy-start = (bf16[768,768]{1,0:T(8,128)(2,1)S(1)}, bf16[768,768]{1,0:T(8,128)(2,1)}, u32[]{:S(2)}) copy-start(bf16[768,768]{1,0:T(8,128)(2,1)} %param.24) | copy-start | bytes 3538948
  7.2 55.3 %reduce-scatter.9.cloned.1.call-start = ((), (), s32[]{:S(2)}) async-start(), calls=%async_computation.11 | async-start | bytes 1966080 | tf_op jit(solution)/shard_map/reduce_scatter | solution.py:160
  31.4 61.9 %reduce-scatter.13.cloned.1.call-start = ((), (), s32[]{:S(2)}) async-start(), calls=%async_computation.14 | async-start | bytes 1966080 | tf_op jit(solution)/shard_map/reduce_scatter | solution.py:160
  45.1 74.4 %all-gather.7.cloned.1.call-start = ((), (), s32[]{:S(2)}) async-start(), calls=%async_computation.15 | async-start | bytes 1966080 | tf_op jit(solution)/shard_map/all_gather | solution.py:168
  49.1 172.4 %copy-start.12 = (bf16[1,1024,768]{2,1,0:T(8,128)(2,1)}, bf16[1,1024,768]{2,1,0:T(8,128)(2,1)S(1)}, u32[]{:S(2)}) copy-start(bf16[1,1024,768]{2,1,0:T(8,128)(2,1)S(1)} %get-tuple-element.84) | copy-start | bytes 4718596
  62.5 34.8 %copy-start.7 = (bf16[256,768]{1,0:T(8,128)(2,1)S(1)}, bf16[256,768]{1,0:T(8,128)(2,1)}, u32[]{:S(2)}) copy-start(bf16[256,768]{1,0:T(8,128)(2,1)} %reduce-scatter.9.cloned.1.call-done) | copy-start | bytes 1179652
  99.7 41.5 %all-gather.5.cloned.1.call-start = ((), (), s32[]{:S(2)}) async-start(), calls=%async_computation.12 | async-start | bytes 1966080 | tf_op jit(solution)/shard_map/all_gather | solution.py:168
  100.3 90.4 %reduce-scatter.11.cloned.1.call-start = ((), (), s32[]{:S(2)}) async-start(), calls=%async_computation.13 | async-start | bytes 1966080 | tf_op jit(solution)/shard_map/reduce_scatter | solution.py:171
  162.4 59.1 %reduce-scatter.15.cloned.1.call-start = ((), (), s32[]{:S(2)}) async-start(), calls=%async_computation.16 | async-start | bytes 1966080 | tf_op jit(solution)/shard_map/reduce_scatter | solution.py:171
  166.8 133.3 %reduce-scatter.17.cloned.1.call-start = ((), (), s32[]{:S(2)}) async-start(), calls=%async_computation.17 | async-start | bytes 1966080 | tf_op jit(solution)/shard_map/reduce_scatter | solution.py:216
  229.5 8.6 %collective-permute-start = (bf16[256,768]{1,0:T(8,128)(2,1)}, bf16[256,768]{1,0:T(8,128)(2,1)}, u32[]{:S(2)}, u32[]{:S(2)}) collective-permute-start(bf16[256,768]{1,0:T(8,128)(2,1)} %get-tuple-element.73), channel_id=1, source_target_pairs={{0,1},{1,2},{2,3},{3,0},{4,5},{5,6},{6,7},{7,4},{8,9},{9,10},{10,1... | collective-permute-start | bytes 1179656 | tf_op jit(solution)/shard_map/ppermute | solution.py:191
  231.8 14.7 %collective-permute-start.3 = (bf16[256,768]{1,0:T(8,128)(2,1)}, bf16[256,768]{1,0:T(8,128)(2,1)}, u32[]{:S(2)}, u32[]{:S(2)}) collective-permute-start(bf16[256,768]{1,0:T(8,128)(2,1)} %get-tuple-element.69), channel_id=1, source_target_pairs={{0,1},{1,2},{2,3},{3,0},{4,5},{5,6},{6,7},{7,4},{8,9},{9,10},{10,1... | collective-permute-start | bytes 1179656 | tf_op jit(solution)/shard_map/ppermute | solution.py:191
  232.2 18.0 %collective-permute-start.1 = (bf16[256,768]{1,0:T(8,128)(2,1)}, bf16[256,768]{1,0:T(8,128)(2,1)}, u32[]{:S(2)}, u32[]{:S(2)}) collective-permute-start(bf16[256,768]{1,0:T(8,128)(2,1)} %get-tuple-element.73), channel_id=1, source_target_pairs={{0,3},{1,0},{2,1},{3,2},{4,7},{5,4},{6,5},{7,6},{8,11},{9,8},{10,9... | collective-permute-start | bytes 1179656 | tf_op jit(solution)/shard_map/ppermute | solution.py:196
  233.6 18.4 %collective-permute-start.4 = (bf16[256,768]{1,0:T(8,128)(2,1)}, bf16[256,768]{1,0:T(8,128)(2,1)}, u32[]{:S(2)}, u32[]{:S(2)}) collective-permute-start(bf16[256,768]{1,0:T(8,128)(2,1)} %get-tuple-element.69), channel_id=1, source_target_pairs={{0,3},{1,0},{2,1},{3,2},{4,7},{5,4},{6,5},{7,6},{8,11},{9,8},{10,9... | collective-permute-start | bytes 1179656 | tf_op jit(solution)/shard_map/ppermute | solution.py:196
  238.1 15.7 %collective-permute-start.2 = (bf16[256,768]{1,0:T(8,128)(2,1)}, bf16[256,768]{1,0:T(8,128)(2,1)S(1)}, u32[]{:S(2)}, u32[]{:S(2)}) collective-permute-start(bf16[256,768]{1,0:T(8,128)(2,1)} %collective-permute-done), channel_id=1, source_target_pairs={{0,1},{1,2},{2,3},{3,0},{4,5},{5,6},{6,7},{7,4},{8,9},{9,10},{10,1... | collective-permute-start | bytes 1179656 | tf_op jit(solution)/shard_map/ppermute | solution.py:191
  246.5 11.4 %collective-permute-start.5 = (bf16[256,768]{1,0:T(8,128)(2,1)}, bf16[256,768]{1,0:T(8,128)(2,1)S(1)}, u32[]{:S(2)}, u32[]{:S(2)}) collective-permute-start(bf16[256,768]{1,0:T(8,128)(2,1)} %collective-permute-done.3), channel_id=1, source_target_pairs={{0,1},{1,2},{2,3},{3,0},{4,5},{5,6},{6,7},{7,4},{8,9},{9,10},{10,1... | collective-permute-start | bytes 1179656 | tf_op jit(solution)/shard_map/ppermute | solution.py:191
  270.3 60.7 %reduce-scatter.21.cloned.1.call-start = ((), (), s32[]{:S(2)}) async-start(), calls=%async_computation.20 | async-start | bytes 1966080 | tf_op jit(solution)/shard_map/reduce_scatter | solution.py:216
  274.4 86.9 %all-gather.9.cloned.1.call-start = ((), (), s32[]{:S(2)}) async-start(), calls=%async_computation.18 | async-start | bytes 1966080 | tf_op jit(solution)/shard_map/all_gather | solution.py:230
  352.0 69.7 %all-to-all-start.2 = ((bf16[8,96,1536]{2,1,0:T(8,128)(2,1)}), bf16[8,96,1536]{2,1,0:T(8,128)(2,1)}, u32[]{:S(2)}, u32[]{:S(2)}) async-start(bf16[8,96,1536]{2,1,0:T(8,128)(2,1)} %bitcast.251), calls=%async_computation.10 | async-start | bytes 4718592 | tf_op jit(solution)/shard_map/all_to_all | solution.py:17
  357.7 23.6 %all-gather.11.cloned.1.call-start = ((), (), s32[]{:S(2)}) async-start(), calls=%async_computation.21 | async-start | bytes 1966080 | tf_op jit(solution)/shard_map/all_gather | solution.py:230
  361.0 162.8 %reduce-scatter.19.cloned.1.call-start = ((), (), s32[]{:S(2)}) async-start(), calls=%async_computation.19 | async-start | bytes 1966080 | tf_op jit(solution)/shard_map/reduce_scatter | solution.py:273
  397.8 127.2 %reduce-scatter.23.cloned.1.call-start = ((), (), s32[]{:S(2)}) async-start(), calls=%async_computation.22 | async-start | bytes 1966080 | tf_op jit(solution)/shard_map/reduce_scatter | solution.py:273
  421.7 15.7 %all-to-all-start.1 = ((bf16[8,24,768]{2,1,0:T(8,128)(2,1)}), bf16[8,24,768]{2,1,0:T(8,128)(2,1)}, u32[]{:S(2)}, u32[]{:S(2)}) async-start(bf16[8,24,768]{2,1,0:T(8,128)(2,1)} %bitcast.292), calls=%async_computation.9 | async-start | bytes 589824 | tf_op jit(solution)/shard_map/all_to_all | solution.py:17
  437.4 84.0 %all-to-all-start = ((bf16[8,96,3,192]{1,3,2,0:T(8,128)(2,1)}), bf16[8,96,3,192]{1,3,2,0:T(8,128)(2,1)}, u32[]{:S(2)}, u32[]{:S(2)}) async-start(bf16[8,96,3,192]{1,3,2,0:T(8,128)(2,1)} %copy.30), calls=%async_computation.8 | async-start | bytes 2359296 | tf_op jit(solution)/shard_map/all_to_all | solution.py:17
  (130 other events, 644.6 us)
Sparse Core Ops, SparseCore 0:
  31.6 30.8 reduce-scatter.8
  65.2 28.1 reduce-scatter.12
  99.8 19.6 all-gather.6
  121.5 19.6 all-gather.4
  162.5 28.1 reduce-scatter.10
  193.3 28.1 reduce-scatter.14
  270.4 29.5 reduce-scatter.16
  302.8 28.1 reduce-scatter.20
  338.2 19.6 all-gather.8
  361.1 20.0 all-gather.10
  397.9 28.1 reduce-scatter.18
  428.7 28.6 reduce-scatter.22
